TPU v7x, 32 devices: a whole 2x2x4 slice. The times are simulated.
32 devices in a mesh: cp: 4 (over y, x), fsdp: 2 (over core), rep: 4 (over z).
Axes of the slice: x: 2, y: 2, z: 4, core: 2. Of those that a mesh axis runs over, the one named last changes fastest.
Arguments:
- tokens: bfloat16 [16, 2048, 768], P(('fsdp', 'rep'), 'cp'), may hold values from -6 to 6
- segments: int32 [16, 2048], P(('fsdp', 'rep')), may hold values from 0 to 3, never falling along the last dimension, each value on 1 to 1024 neighbouring positions
- g_one: bfloat16 [768], P('fsdp'), may hold values from 0.099609375 to 1.8984375
- b_one: bfloat16 [768], P('fsdp'), may hold values from -3 to 3
- w_qkv: bfloat16 [768, 2304], P('fsdp'), may hold values from -0.21875 to 0.21875
- b_query: bfloat16 [768], P('fsdp'), may hold values from -3 to 3
- b_value: bfloat16 [768], P('fsdp'), may hold values from -3 to 3
- w_out: bfloat16 [768, 768], P('fsdp'), may hold values from -1.75 to 1.75
- b_out: bfloat16 [768], P('fsdp'), may hold values from -3 to 3
- g_two: bfloat16 [768], P('fsdp'), may hold values from 0.099609375 to 1.8984375
- b_two: bfloat16 [768], P('fsdp'), may hold values from -3 to 3
- w_fc: bfloat16 [768, 3072], P('fsdp'), may hold values from -0.21875 to 0.21875
- b_fc: bfloat16 [3072], P('fsdp'), may hold values from -3 to 3
- w_proj: bfloat16 [3072, 768], P('fsdp'), may hold values from -0.109375 to 0.109375
- b_proj: bfloat16 [768], P('fsdp'), may hold values from -3 to 3
- cotangent: bfloat16 [16, 2048, 768], P(('fsdp', 'rep'), 'cp'), may hold values from -6 to 6
Outputs:
- layer_out: bfloat16 [16, 2048, 768], P(('fsdp', 'rep'), 'cp')
- tokens_grad: bfloat16 [16, 2048, 768], P(('fsdp', 'rep'), 'cp')
- dg_one: float32 [768], P('fsdp')
- db_one: float32 [768], P('fsdp')
- dw_qkv: float32 [768, 2304], P('fsdp')
- db_query: float32 [768], P('fsdp')
- db_value: float32 [768], P('fsdp')
- dw_out: float32 [768, 768], P('fsdp')
- db_out: float32 [768], P('fsdp')
- dg_two: float32 [768], P('fsdp')
- db_two: float32 [768], P('fsdp')
- dw_fc: float32 [768, 3072], P('fsdp')
- db_fc: float32 [3072], P('fsdp')
- dw_proj: float32 [3072, 768], P('fsdp')
- db_proj: float32 [768], P('fsdp')
Inputs may be any that keep to these rules, and one draw needn't show every extreme that they name: `segments`: in each sequence the ids never fall, and each document holds 1 to 1024 positions, one document exactly that many.
All inputs are finite; a program needn't handle non-finite values.
Results may differ from a plain program's by a relative error of at most 0.012.
The roundings to bfloat16 on the way count: a program that leaves them out, or rounds other values in their place, can miss the bound.
Values may be sent and summed in bfloat16 or wider, within the bound.
A program may use at most 384 MiB of HBM per device.

v0:
```python
import jax
import jax.numpy as jnp
from jax import lax
from jax.sharding import PartitionSpec as P

HEADS = 12


def layer_norm(value, gain, shift):
    center = value - jnp.mean(value, axis=-1, keepdims=True)
    spread = jnp.mean(center * center, axis=-1, keepdims=True)
    return center * lax.rsqrt(spread + 1e-05) * gain + shift


def gelu_tanh(value):
    return (
        0.5
        * value
        * (1.0 + jnp.tanh(0.7978845608028654 * (value + 0.044715 * value * value * value)))
    )


def inner_rows(left, right):
    return lax.dot_general(
        left, right, (((0,), (0,)), ((), ())), preferred_element_type=jnp.float32
    )


def times_trans(left, right):
    return lax.dot_general(
        left, right, (((1,), (1,)), ((), ())), preferred_element_type=jnp.float32
    )


def body(
    tokens,
    segments,
    g_one,
    b_one,
    w_qkv,
    b_query,
    b_value,
    w_out,
    b_out,
    g_two,
    b_two,
    w_fc,
    b_fc,
    w_proj,
    b_proj,
    cotangent,
):
    seqs, span, width = tokens.shape
    seq_len = segments.shape[1]
    rows = seqs * span
    size = width // HEADS
    scale = size ** (-0.5)
    first_pos = lax.axis_index("cp") * span
    full = (
        lax.all_gather(g_one, "fsdp", axis=0, tiled=True),
        lax.all_gather(b_one, "fsdp", axis=0, tiled=True),
        lax.all_gather(w_qkv, "fsdp", axis=0, tiled=True),
        lax.all_gather(b_query, "fsdp", axis=0, tiled=True),
        lax.all_gather(b_value, "fsdp", axis=0, tiled=True),
        lax.all_gather(w_out, "fsdp", axis=0, tiled=True),
        lax.all_gather(b_out, "fsdp", axis=0, tiled=True),
        lax.all_gather(g_two, "fsdp", axis=0, tiled=True),
        lax.all_gather(b_two, "fsdp", axis=0, tiled=True),
        lax.all_gather(w_fc, "fsdp", axis=0, tiled=True),
        lax.all_gather(b_fc, "fsdp", axis=0, tiled=True),
        lax.all_gather(w_proj, "fsdp", axis=0, tiled=True),
        lax.all_gather(b_proj, "fsdp", axis=0, tiled=True),
    )
    gain_one = full[0].astype(jnp.float32)
    shift_one = full[1].astype(jnp.float32)
    gain_two = full[7].astype(jnp.float32)
    shift_two = full[8].astype(jnp.float32)
    tok_rows = tokens.reshape(rows, width).astype(jnp.float32)
    normed = layer_norm(tok_rows, gain_one, shift_one).astype(jnp.bfloat16)
    qkv_bias = jnp.concatenate([full[3], jnp.zeros_like(full[3]), full[4]]).astype(jnp.float32)
    merged = (jnp.dot(normed, full[2], preferred_element_type=jnp.float32) + qkv_bias).astype(
        jnp.bfloat16
    )
    merged = merged.reshape(seqs, span, 3 * width)
    query = merged[:, :, :width]
    key_loc = merged[:, :, width : 2 * width]
    value_loc = merged[:, :, 2 * width :]
    keys_all, values_all = (
        lax.all_gather(key_loc, "cp", axis=1, tiled=True),
        lax.all_gather(value_loc, "cp", axis=1, tiled=True),
    )
    key_pos = jnp.arange(seq_len)

    def masked_scores(q_rows, k_rows, seq_ids, near_ids):
        length = k_rows.shape[0]
        q_three = q_rows.reshape(span, HEADS, size)
        k_three = k_rows.reshape(length, HEADS, size)
        scores = (
            jnp.einsum("qhd,khd->hqk", q_three, k_three, preferred_element_type=jnp.float32) * scale
        )
        query_ids = lax.dynamic_slice_in_dim(seq_ids, first_pos, span)
        query_pos = first_pos + jnp.arange(span)
        allowed = (query_ids[:, None] == near_ids[None, :]) & (
            key_pos[None, :] <= query_pos[:, None]
        )
        return jnp.where(allowed[None], scores, -1e30)

    def attend(item):
        q_rows, k_rows, v_rows, seq_ids, near_ids = item
        length = k_rows.shape[0]
        scores = masked_scores(q_rows, k_rows, seq_ids, near_ids)
        top = jnp.max(scores, axis=-1, keepdims=True)
        expo = jnp.exp(scores - top)
        total = jnp.sum(expo, axis=-1, keepdims=True)
        probs = (expo / total).astype(jnp.bfloat16)
        mixed = jnp.einsum(
            "hqk,khd->qhd",
            probs,
            v_rows.reshape(length, HEADS, size),
            preferred_element_type=jnp.float32,
        )
        return (
            mixed.reshape(span, width).astype(jnp.bfloat16),
            top[..., 0] + jnp.log(total[..., 0]),
        )

    mixed, log_total = lax.map(attend, (query, keys_all, values_all, segments, segments))
    mixed_rows = mixed.reshape(rows, width)
    branch = jnp.dot(mixed_rows, full[5], preferred_element_type=jnp.float32) + full[6].astype(
        jnp.float32
    )
    resid = tok_rows + branch
    normed_two = layer_norm(resid, gain_two, shift_two).astype(jnp.bfloat16)
    hidden = jnp.dot(normed_two, full[9], preferred_element_type=jnp.float32) + full[10].astype(
        jnp.float32
    )
    active = gelu_tanh(hidden).astype(jnp.bfloat16)
    output = jnp.dot(active, full[11], preferred_element_type=jnp.float32) + full[12].astype(
        jnp.float32
    )
    layer_out = (resid + output).astype(jnp.bfloat16).reshape(seqs, span, width)
    back = (
        lax.all_gather(g_one, "fsdp", axis=0, tiled=True),
        lax.all_gather(b_one, "fsdp", axis=0, tiled=True),
        lax.all_gather(w_qkv, "fsdp", axis=0, tiled=True),
        lax.all_gather(b_query, "fsdp", axis=0, tiled=True),
        lax.all_gather(b_value, "fsdp", axis=0, tiled=True),
        lax.all_gather(w_out, "fsdp", axis=0, tiled=True),
        lax.all_gather(b_out, "fsdp", axis=0, tiled=True),
        lax.all_gather(g_two, "fsdp", axis=0, tiled=True),
        lax.all_gather(b_two, "fsdp", axis=0, tiled=True),
        lax.all_gather(w_fc, "fsdp", axis=0, tiled=True),
        lax.all_gather(b_fc, "fsdp", axis=0, tiled=True),
        lax.all_gather(w_proj, "fsdp", axis=0, tiled=True),
        lax.all_gather(b_proj, "fsdp", axis=0, tiled=True),
    )
    keys_b, values_b = (
        lax.all_gather(key_loc, "cp", axis=1, tiled=True),
        lax.all_gather(value_loc, "cp", axis=1, tiled=True),
    )
    out_grad = cotangent.reshape(rows, width).astype(jnp.float32)
    d_output = out_grad.astype(jnp.bfloat16)
    dw_proj = inner_rows(active, d_output)
    db_proj = jnp.sum(d_output.astype(jnp.float32), axis=0)
    d_active = times_trans(d_output, back[11])
    _, gelu_pull = jax.vjp(gelu_tanh, hidden)
    d_hidden = gelu_pull(d_active)[0].astype(jnp.bfloat16)
    dw_fc = inner_rows(normed_two, d_hidden)
    db_fc = jnp.sum(d_hidden.astype(jnp.float32), axis=0)
    d_normed_two = times_trans(d_hidden, back[9])
    _, norm_pull_two = jax.vjp(
        layer_norm, resid, back[7].astype(jnp.float32), back[8].astype(jnp.float32)
    )
    d_resid_part, dg_two, db_two = norm_pull_two(d_normed_two)
    d_resid = out_grad + d_resid_part
    d_branch = d_resid.astype(jnp.bfloat16)
    dw_out = inner_rows(mixed_rows, d_branch)
    db_out = jnp.sum(d_branch.astype(jnp.float32), axis=0)
    d_mixed = times_trans(d_branch, back[5]).astype(jnp.bfloat16).reshape(seqs, span, width)

    def attend_back(item):
        q_rows, k_rows, v_rows, seq_ids, near_ids, d_rows, lse_rows = item
        length = k_rows.shape[0]
        scores = masked_scores(q_rows, k_rows, seq_ids, near_ids)
        probs = jnp.exp(scores - lse_rows[..., None])
        d_three = d_rows.reshape(span, HEADS, size)
        v_three = v_rows.reshape(length, HEADS, size)
        d_probs = jnp.einsum("qhd,khd->hqk", d_three, v_three, preferred_element_type=jnp.float32)
        delta = jnp.sum(probs * d_probs, axis=-1, keepdims=True)
        d_scores = (probs * (d_probs - delta)).astype(jnp.bfloat16)
        d_query = (
            jnp.einsum(
                "hqk,khd->qhd",
                d_scores,
                k_rows.reshape(length, HEADS, size),
                preferred_element_type=jnp.float32,
            )
            * scale
        )
        d_key = (
            jnp.einsum(
                "hqk,qhd->khd",
                d_scores,
                q_rows.reshape(span, HEADS, size),
                preferred_element_type=jnp.float32,
            )
            * scale
        )
        d_value = jnp.einsum(
            "hqk,qhd->khd", probs.astype(jnp.bfloat16), d_three, preferred_element_type=jnp.float32
        )
        return (
            d_query.reshape(span, width),
            d_key.reshape(length, width),
            d_value.reshape(length, width),
        )

    d_query, d_key_all, d_value_all = lax.map(
        attend_back, (query, keys_b, values_b, segments, segments, d_mixed, log_total)
    )
    d_key, d_value = (
        lax.psum_scatter(d_key_all, "cp", scatter_dimension=1, tiled=True),
        lax.psum_scatter(d_value_all, "cp", scatter_dimension=1, tiled=True),
    )
    d_merged = (
        jnp.concatenate([d_query, d_key, d_value], axis=-1)
        .astype(jnp.bfloat16)
        .reshape(rows, 3 * width)
    )
    d_merged_f = d_merged.astype(jnp.float32)
    db_query = jnp.sum(d_merged_f[:, :width], axis=0)
    db_value = jnp.sum(d_merged_f[:, 2 * width :], axis=0)
    dw_qkv = inner_rows(normed, d_merged)
    d_normed = times_trans(d_merged, back[2])
    _, norm_pull_one = jax.vjp(
        layer_norm, tok_rows, back[0].astype(jnp.float32), back[1].astype(jnp.float32)
    )
    d_tok_part, dg_one, db_one = norm_pull_one(d_normed)
    tokens_grad = (d_resid + d_tok_part).astype(jnp.bfloat16).reshape(seqs, span, width)
    shards = (
        lax.psum_scatter(dg_one, "fsdp", scatter_dimension=0, tiled=True),
        lax.psum_scatter(db_one, "fsdp", scatter_dimension=0, tiled=True),
        lax.psum_scatter(dw_qkv, "fsdp", scatter_dimension=0, tiled=True),
        lax.psum_scatter(db_query, "fsdp", scatter_dimension=0, tiled=True),
        lax.psum_scatter(db_value, "fsdp", scatter_dimension=0, tiled=True),
        lax.psum_scatter(dw_out, "fsdp", scatter_dimension=0, tiled=True),
        lax.psum_scatter(db_out, "fsdp", scatter_dimension=0, tiled=True),
        lax.psum_scatter(dg_two, "fsdp", scatter_dimension=0, tiled=True),
        lax.psum_scatter(db_two, "fsdp", scatter_dimension=0, tiled=True),
        lax.psum_scatter(dw_fc, "fsdp", scatter_dimension=0, tiled=True),
        lax.psum_scatter(db_fc, "fsdp", scatter_dimension=0, tiled=True),
        lax.psum_scatter(dw_proj, "fsdp", scatter_dimension=0, tiled=True),
        lax.psum_scatter(db_proj, "fsdp", scatter_dimension=0, tiled=True),
    )
    totals = lax.psum(
        (
            shards[0],
            shards[1],
            shards[2],
            shards[3],
            shards[4],
            shards[5],
            shards[6],
            shards[7],
            shards[8],
            shards[9],
            shards[10],
            shards[11],
            shards[12],
        ),
        ("cp", "rep"),
    )
    return (
        layer_out,
        tokens_grad,
        totals[0],
        totals[1],
        totals[2],
        totals[3],
        totals[4],
        totals[5],
        totals[6],
        totals[7],
        totals[8],
        totals[9],
        totals[10],
        totals[11],
        totals[12],
    )


def solution(mesh):
    placed = (
        P(("fsdp", "rep"), "cp", None),
        P(("fsdp", "rep"), None),
        P("fsdp"),
        P("fsdp"),
        P("fsdp", None),
        P("fsdp"),
        P("fsdp"),
        P("fsdp", None),
        P("fsdp"),
        P("fsdp"),
        P("fsdp"),
        P("fsdp", None),
        P("fsdp"),
        P("fsdp", None),
        P("fsdp"),
        P(("fsdp", "rep"), "cp", None),
    )
    return jax.shard_map(
        body,
        mesh=mesh,
        in_specs=placed,
        out_specs=(
            P(("fsdp", "rep"), "cp", None),
            P(("fsdp", "rep"), "cp", None),
            P("fsdp"),
            P("fsdp"),
            P("fsdp", None),
            P("fsdp"),
            P("fsdp"),
            P("fsdp", None),
            P("fsdp"),
            P("fsdp"),
            P("fsdp"),
            P("fsdp", None),
            P("fsdp"),
            P("fsdp", None),
            P("fsdp"),
        ),
        check_vma=False,
    )
```

profile of v0, /device:TPU:0, one launch (start us, length us, event | category | flops | bytes accessed | tf_op | source)
XLA Modules:
  0.0 1499.2 jit_solution(1097224443274911993)
XLA Ops:
  50.4 56.1 %all-gather.20.cloned.1.call-done = bf16[2,2048,768]{1,2,0:T(8,128)(2,1)} async-done(((bf16[2,512,768]{1,2,0:T(8,128)(2,1)}), bf16[2,2048,768]{1,2,0:T(8,128)(2,1)}) %all-gather.20.cloned.1.call-update) | async-done | bytes 6291472 | tf_op jit(solution)/shard_map/all_gather | solution.py:89
  106.5 72.5 %all-gather.18.cloned.1.call-done = bf16[2,2048,768]{1,2,0:T(8,128)(2,1)} async-done(((bf16[2,512,768]{1,2,0:T(8,128)(2,1)}), bf16[2,2048,768]{1,2,0:T(8,128)(2,1)}) %all-gather.18.cloned.1.call-update) | async-done | bytes 6291472 | tf_op jit(solution)/shard_map/all_gather | solution.py:90
  178.9 155.2 %while.34 = (s32[]{:T(128)}, bf16[2,512,768]{2,1,0:T(8,128)(2,1)}, f32[2,12,512]{2,1,0:T(8,128)S(1)}, bf16[2,2048,768]{1,2,0:T(8,128)(2,1)}, s32[2,2048]{1,0:T(2...) while((s32[]{:T(128)}, bf16[2,512,768]{2,1,0:T(8,128)(2,1)}, ...), condition=%wide.region_5.6_spmd.clone, body=%wide.region_2.5_spmd.clone.sunk | while | flops 3375753728 | bytes 197388496 | solution.py:127
  188.6 23.9 %fusion.106 = (f32[12,512]{1,0:T(8,128)S(1)}, f32[12,512,2048]{2,1,0:T(8,128)}) fusion(pred[512,2048]{1,0:T(8,128)(4,1)} %fusion.105, bf16[512,12,64]{0,2,1:T(8,128)(2,1)} %bitcast.170, bf16[2048,12,64]{0,2,1:T(8,128)(2,1)S(1)} %bitcast.165), kind=kOutput, calls=%fused_computation.5.clone.1 | convolution fusion | flops 1648355328 | bytes 55336960 | tf_op jit(solution)/shard_map/while/body/eval_jaxpr/qhd,khd->hqk/dot_general | solution.py:99
  212.5 24.5 %fusion.107 = f32[12,512]{1,0:T(8,128)S(1)} fusion(f32[12,512,2048]{2,1,0:T(8,128)} %get-tuple-element.683, f32[12,512]{1,0:T(8,128)S(1)} %get-tuple-element.684, pred[512,2048]{1,0:T(8,128)(4,1)} %fusion.105), kind=kLoop, calls=%fused_computation.6.clone.1 | loop fusion | flops 50325504 | bytes 51429376 | tf_op jit(solution)/shard_map/while/body/eval_jaxpr/reduce_sum | solution.py:114
  237.1 20.2 %fusion.108 = bf16[12,64,512]{2,1,0:T(8,128)(2,1)S(1)} fusion(bf16[2048,12,64]{0,2,1:T(8,128)(2,1)S(1)} %bitcast.174, f32[12,512,2048]{2,1,0:T(8,128)} %get-tuple-element.683, f32[12,512]{1,0:T(8,128)S(1)} %fusion.107, f32[12,512]{1,0:T(8,128)S(1)} %get-tuple-element.684, pred[512,2048]{1,0:T(8,128)(4,1)S(1)} %copy-done), kind=kOutput, calls=%fused_computation.10.clone.1 | convolution fusion | flops 1673920512 | bytes 55361536 | tf_op jit(solution)/shard_map/while/body/eval_jaxpr/hqk,khd->qhd/dot_general | solution.py:116
  268.2 21.5 %fusion.106 = (f32[12,512]{1,0:T(8,128)S(1)}, f32[12,512,2048]{2,1,0:T(8,128)}) fusion(pred[512,2048]{1,0:T(8,128)(4,1)} %fusion.105, bf16[512,12,64]{0,2,1:T(8,128)(2,1)} %bitcast.170, bf16[2048,12,64]{0,2,1:T(8,128)(2,1)S(1)} %bitcast.165), kind=kOutput, calls=%fused_computation.5.clone.1 | convolution fusion | flops 1648355328 | bytes 55336960 | tf_op jit(solution)/shard_map/while/body/eval_jaxpr/qhd,khd->hqk/dot_general | solution.py:99
  289.7 22.9 %fusion.107 = f32[12,512]{1,0:T(8,128)S(1)} fusion(f32[12,512,2048]{2,1,0:T(8,128)} %get-tuple-element.683, f32[12,512]{1,0:T(8,128)S(1)} %get-tuple-element.684, pred[512,2048]{1,0:T(8,128)(4,1)} %fusion.105), kind=kLoop, calls=%fused_computation.6.clone.1 | loop fusion | flops 50325504 | bytes 51429376 | tf_op jit(solution)/shard_map/while/body/eval_jaxpr/reduce_sum | solution.py:114
  312.5 20.2 %fusion.108 = bf16[12,64,512]{2,1,0:T(8,128)(2,1)S(1)} fusion(bf16[2048,12,64]{0,2,1:T(8,128)(2,1)S(1)} %bitcast.174, f32[12,512,2048]{2,1,0:T(8,128)} %get-tuple-element.683, f32[12,512]{1,0:T(8,128)S(1)} %fusion.107, f32[12,512]{1,0:T(8,128)S(1)} %get-tuple-element.684, pred[512,2048]{1,0:T(8,128)(4,1)S(1)} %copy-done), kind=kOutput, calls=%fused_computation.10.clone.1 | convolution fusion | flops 1673920512 | bytes 55361536 | tf_op jit(solution)/shard_map/while/body/eval_jaxpr/hqk,khd->qhd/dot_general | solution.py:116
  379.7 375.4 %while.35 = (s32[]{:T(128)}, bf16[2,512,768]{2,1,0:T(8,128)(2,1)}, f32[2,2048,768]{2,1,0:T(8,128)}, f32[2,2048,768]{2,1,0:T(8,128)}, bf16[2,2048,768]{1,2,0:T(8,...) while((s32[]{:T(128)}, bf16[2,512,768]{2,1,0:T(8,128)(2,1)}, ...), condition=%wide.region_12.13_spmd.clone, body=%wide.region_10.12_spmd.clone.sunk | while | flops 8247306752 | bytes 519514368 | solution.py:218
  392.5 20.5 %fusion.119 = f32[12,512,2048]{2,1,0:T(8,128)} fusion(bf16[512,12,64]{0,2,1:T(8,128)(2,1)} %bitcast.167, bf16[2048,12,64]{0,2,1:T(8,128)(2,1)S(1)} %bitcast.162), kind=kOutput, calls=%fused_computation.114.clone.1 | convolution fusion | flops 1610612736 | bytes 54263808 | tf_op jit(solution)/shard_map/while/body/eval_jaxpr/qhd,khd->hqk/dot_general | solution.py:99
  413.0 23.1 %fusion.121 = f32[12,64,2048]{2,1,0:T(8,128)} fusion(bf16[512,12,64]{0,2,1:T(8,128)(2,1)} %bitcast.172, f32[12,512,2048]{2,1,0:T(8,128)} %fusion.119, f32[12,512]{1,0:T(8,128)S(1)} %dynamic-slice_bitcast_fusion.2, pred[512,2048]{1,0:T(8,128)(4,1)} %fusion.120), kind=kOutput, calls=%fused_computation.24.clone.1 | convolution fusion | flops 1660944384 | bytes 58482688 | tf_op jit(solution)/shard_map/while/body/eval_jaxpr/hqk,qhd->khd/dot_general | solution.py:209
  442.7 37.6 %multiply_reduce_fusion.5 = (f32[12,512]{1,0:T(8,128)S(1)}, f32[12,512,2048]{2,1,0:T(8,128)}) fusion(f32[12,512,2048]{2,1,0:T(8,128)} %fusion.119, f32[12,512]{1,0:T(8,128)S(1)} %dynamic-slice_bitcast_fusion.2, pred[512,2048]{1,0:T(8,128)(4,1)} %fusion.120, bf16[512,12,64]{0,2,1:T(8,128)(2,1)} %bitcast.173, bf16[2048,12,64]{0,2,1:T(8,128)(2,1)} %bitcast.166), kind=kOutput, calls=%fused_computation.21.clone.1 | convolution fusion | flops 1673521152 | bytes 105693184 | tf_op jit(solution)/shard_map/while/body/eval_jaxpr/qhd,khd->hqk/dot_general | solution.py:188
  480.3 41.4 %multiply_convert_fusion.5 = bf16[12,512,2048]{2,1,0:T(8,128)(2,1)} fusion(f32[12,512,2048]{2,1,0:T(8,128)} %get-tuple-element.697, f32[12,512,2048]{2,1,0:T(8,128)} %fusion.119, f32[12,512]{1,0:T(8,128)S(1)} %get-tuple-element.698, f32[12,512]{1,0:T(8,128)S(1)} %dynamic-slice_bitcast_fusion.2, pred[512,2048]{1,0:T(8,128)(4,1)} %fusion.120), kind=kLoop, calls=%fused_computation.20.clone.1 | loop fusion | flops 75497472 | bytes 126926848 | tf_op jit(solution)/shard_map/while/body/eval_jaxpr/convert_element_type | solution.py:190
  578.6 20.5 %fusion.119 = f32[12,512,2048]{2,1,0:T(8,128)} fusion(bf16[512,12,64]{0,2,1:T(8,128)(2,1)} %bitcast.167, bf16[2048,12,64]{0,2,1:T(8,128)(2,1)S(1)} %bitcast.162), kind=kOutput, calls=%fused_computation.114.clone.1 | convolution fusion | flops 1610612736 | bytes 54263808 | tf_op jit(solution)/shard_map/while/body/eval_jaxpr/qhd,khd->hqk/dot_general | solution.py:99
  599.1 23.1 %fusion.121 = f32[12,64,2048]{2,1,0:T(8,128)} fusion(bf16[512,12,64]{0,2,1:T(8,128)(2,1)} %bitcast.172, f32[12,512,2048]{2,1,0:T(8,128)} %fusion.119, f32[12,512]{1,0:T(8,128)S(1)} %dynamic-slice_bitcast_fusion.2, pred[512,2048]{1,0:T(8,128)(4,1)} %fusion.120), kind=kOutput, calls=%fused_computation.24.clone.1 | convolution fusion | flops 1660944384 | bytes 58482688 | tf_op jit(solution)/shard_map/while/body/eval_jaxpr/hqk,qhd->khd/dot_general | solution.py:209
  628.9 37.6 %multiply_reduce_fusion.5 = (f32[12,512]{1,0:T(8,128)S(1)}, f32[12,512,2048]{2,1,0:T(8,128)}) fusion(f32[12,512,2048]{2,1,0:T(8,128)} %fusion.119, f32[12,512]{1,0:T(8,128)S(1)} %dynamic-slice_bitcast_fusion.2, pred[512,2048]{1,0:T(8,128)(4,1)} %fusion.120, bf16[512,12,64]{0,2,1:T(8,128)(2,1)} %bitcast.173, bf16[2048,12,64]{0,2,1:T(8,128)(2,1)} %bitcast.166), kind=kOutput, calls=%fused_computation.21.clone.1 | convolution fusion | flops 1673521152 | bytes 105693184 | tf_op jit(solution)/shard_map/while/body/eval_jaxpr/qhd,khd->hqk/dot_general | solution.py:188
  666.4 41.4 %multiply_convert_fusion.5 = bf16[12,512,2048]{2,1,0:T(8,128)(2,1)} fusion(f32[12,512,2048]{2,1,0:T(8,128)} %get-tuple-element.697, f32[12,512,2048]{2,1,0:T(8,128)} %fusion.119, f32[12,512]{1,0:T(8,128)S(1)} %get-tuple-element.698, f32[12,512]{1,0:T(8,128)S(1)} %dynamic-slice_bitcast_fusion.2, pred[512,2048]{1,0:T(8,128)(4,1)} %fusion.120), kind=kLoop, calls=%fused_computation.20.clone.1 | loop fusion | flops 75497472 | bytes 126926848 | tf_op jit(solution)/shard_map/while/body/eval_jaxpr/convert_element_type | solution.py:190
  787.2 88.8 %reduce-scatter.9.cloned.1.call-done = f32[2,512,768]{2,1,0:T(8,128)} async-done(((f32[2,2048,768]{2,1,0:T(8,128)}), f32[2,512,768]{2,1,0:T(8,128)}) %reduce-scatter.9.cloned.1.call-update) | async-done | bytes 3145744 | tf_op jit(solution)/shard_map/reduce_scatter | solution.py:223
  878.1 121.8 %reduce-scatter.7.cloned.1.call-done = f32[2,512,768]{2,1,0:T(8,128)} async-done(((f32[2,2048,768]{2,1,0:T(8,128)}), f32[2,512,768]{2,1,0:T(8,128)}) %reduce-scatter.7.cloned.1.call-update) | async-done | bytes 3145744 | tf_op jit(solution)/shard_map/reduce_scatter | solution.py:222
  1012.7 21.2 %reduce-scatter.15.cloned.1.call-done = f32[384,3072]{1,0:T(8,128)} async-done(((f32[768,3072]{1,0:T(8,128)}), f32[384,3072]{1,0:T(8,128)}) %reduce-scatter.15.cloned.1.call-update) | async-done | bytes 4718608 | tf_op jit(solution)/shard_map/reduce_scatter | solution.py:250
  1033.9 21.5 %reduce-scatter.17.cloned.1.call-done = f32[1536,768]{1,0:T(8,128)} async-done(((f32[3072,768]{1,0:T(8,128)}), f32[1536,768]{1,0:T(8,128)}) %reduce-scatter.17.cloned.1.call-update) | async-done | bytes 4718608 | tf_op jit(solution)/shard_map/reduce_scatter | solution.py:252
  1108.0 82.4 %all-reduce.9 = (f32[384]{0:T(512)}, f32[384]{0:T(512)}, f32[384]{0:T(512)}, f32[384]{0:T(512)}, f32[384]{0:T(512)}, /*index=5*/f32[384]{0:T(512)}, f32[384]{0:T(512)}, f32[1536]{0:T(1024)}, f32[384]{0:T(512)}) all-reduce(f32[384]{0:T(512)S(1)} %dynamic-slice.11, ...), channel_id=1, replica_groups=mesh['cp'=4,'fsdp'=2,'rep'=4] {'cp','rep'}, use_global_device_ids=true, to_apply=%region_19.20 | all-reduce | flops 4608 | bytes 36864 | tf_op jit(solution)/shard_map/psum | solution.py:255
  1195.0 286.7 %all-reduce.14.cloned.1.call-done = (f32[384,2304]{1,0:T(8,128)}, f32[384,768]{1,0:T(8,128)}, f32[384,3072]{1,0:T(8,128)}, f32[1536,768]{1,0:T(8,128)}) async-done(((f32[384,2304]{1,0:T(8,128)}, f32[384,768]{1,0:T(8,128)}, f32[384,3072]{1,0:T(8,128)}, f32[1536,768]{1,0:T(8,128)}), (f32[384,2304]{1,0:T(8,128)}, f32[384,768]{1,0:T(8,128)}, f32[384,3072]{1,0:T(8,128)}, ...) | async-done | bytes 14155792 | tf_op jit(solution)/shard_map/psum | solution.py:255
  (319 shorter events, 350.1 us)
Async XLA Ops:
  7.2 17.8 %all-gather.16.cloned.1.call-start = ((), (), s32[]{:S(2)}) async-start(), calls=%async_computation.6 | async-start | bytes 5308416 | tf_op jit(solution)/shard_map/all_gather | solution.py:62
  7.9 98.5 %all-gather.20.cloned.1.call-start = ((), (), s32[]{:S(2)}) async-start(), calls=%async_computation.8 | async-start | bytes 7864320 | tf_op jit(solution)/shard_map/all_gather | solution.py:89
  35.1 143.8 %all-gather.18.cloned.1.call-start = ((), (), s32[]{:S(2)}) async-start(), calls=%async_computation.7 | async-start | bytes 7864320 | tf_op jit(solution)/shard_map/all_gather | solution.py:90
  36.8 297.3 %all-gather.22.cloned.1.call-start = ((), (), s32[]{:S(2)}) async-start(), calls=%async_computation.9 | async-start | bytes 1769472 | tf_op jit(solution)/shard_map/all_gather | solution.py:65
  37.4 141.6 %copy-start.23 = (s32[2,2048]{1,0:T(2,128)S(1)}, s32[2,2048]{1,0:T(2,128)}, u32[]{:S(2)}) copy-start(s32[2,2048]{1,0:T(2,128)} %param.21) | copy-start | bytes 49156
  37.4 301.1 %all-gather.24.cloned.1.call-start = ((), (), s32[]{:S(2)}) async-start(), calls=%async_computation.10 | async-start | bytes 7077888 | tf_op jit(solution)/shard_map/all_gather | solution.py:69
  38.0 311.6 %all-gather.26.cloned.1.call-start = ((), (), s32[]{:S(2)}) async-start(), calls=%async_computation.11 | async-start | bytes 7077888 | tf_op jit(solution)/shard_map/all_gather | solution.py:71
  38.5 837.5 %reduce-scatter.9.cloned.1.call-start = ((), (), s32[]{:S(2)}) async-start(), calls=%async_computation.13 | async-start | bytes 15728640 | tf_op jit(solution)/shard_map/reduce_scatter | solution.py:223
  178.9 155.2 %copy-start.46 = (f32[768]{0:T(1024)S(1)}, f32[768]{0:T(1024)}, u32[]{:S(2)}) copy-start(f32[768]{0:T(1024)} %reshape.447) | copy-start | bytes 9220
  212.5 24.5 %copy-start = (pred[512,2048]{1,0:T(8,128)(4,1)S(1)}, pred[512,2048]{1,0:T(8,128)(4,1)}, u32[]{:S(2)}) copy-start(pred[512,2048]{1,0:T(8,128)(4,1)} %fusion.105) | copy-start | bytes 3145732 | tf_op jit(solution)/shard_map/while
  212.5 24.5 %copy-start.3 = (bf16[1,2048,768]{1,2,0:T(8,128)(2,1)S(1)}, bf16[1,2048,768]{1,2,0:T(8,128)(2,1)}, u32[]{:S(2)}) copy-start(bf16[1,2048,768]{1,2,0:T(8,128)(2,1)} %get-tuple-element.681) | copy-start | bytes 9437188 | tf_op jit(solution)/shard_map/while
  289.6 22.9 %copy-start = (pred[512,2048]{1,0:T(8,128)(4,1)S(1)}, pred[512,2048]{1,0:T(8,128)(4,1)}, u32[]{:S(2)}) copy-start(pred[512,2048]{1,0:T(8,128)(4,1)} %fusion.105) | copy-start | bytes 3145732 | tf_op jit(solution)/shard_map/while
  289.6 22.9 %copy-start.3 = (bf16[1,2048,768]{1,2,0:T(8,128)(2,1)S(1)}, bf16[1,2048,768]{1,2,0:T(8,128)(2,1)}, u32[]{:S(2)}) copy-start(bf16[1,2048,768]{1,2,0:T(8,128)(2,1)} %get-tuple-element.681) | copy-start | bytes 9437188 | tf_op jit(solution)/shard_map/while
  337.9 36.6 %copy-start.6 = (f32[1024,768]{1,0:T(8,128)}, f32[1024,768]{1,0:T(8,128)S(1)}, u32[]{:S(2)}) copy-start(f32[1024,768]{1,0:T(8,128)S(1)} %get-tuple-element.552) | copy-start | bytes 9437188
  338.0 36.6 %copy-start.24 = (f32[1024]{0:T(1024)}, f32[1024]{0:T(1024)S(1)}, u32[]{:S(2)}) copy-start(f32[1024]{0:T(1024)S(1)} %broadcast_multiply_fusion) | copy-start | bytes 12292
  338.5 36.1 %copy-start.26 = (f32[1024]{0:T(1024)}, f32[1024]{0:T(1024)S(1)}, u32[]{:S(2)}) copy-start(f32[1024]{0:T(1024)S(1)} %fusion.36) | copy-start | bytes 12292
  755.1 244.8 %reduce-scatter.7.cloned.1.call-start = ((), (), s32[]{:S(2)}) async-start(), calls=%async_computation.12 | async-start | bytes 15728640 | tf_op jit(solution)/shard_map/reduce_scatter | solution.py:222
  755.9 256.8 %reduce-scatter.13.cloned.1.call-start = ((), (), s32[]{:S(2)}) async-start(), calls=%async_computation.15 | async-start | bytes 3538944 | tf_op jit(solution)/shard_map/reduce_scatter | solution.py:246
  760.9 273.0 %reduce-scatter.15.cloned.1.call-start = ((), (), s32[]{:S(2)}) async-start(), calls=%async_computation.16 | async-start | bytes 14155776 | tf_op jit(solution)/shard_map/reduce_scatter | solution.py:250
  772.6 282.7 %reduce-scatter.17.cloned.1.call-start = ((), (), s32[]{:S(2)}) async-start(), calls=%async_computation.17 | async-start | bytes 14155776 | tf_op jit(solution)/shard_map/reduce_scatter | solution.py:252
  787.0 287.5 %reduce-scatter.11.cloned.1.call-start = ((), (), s32[]{:S(2)}) async-start(), calls=%async_computation.14 | async-start | bytes 10616832 | tf_op jit(solution)/shard_map/reduce_scatter | solution.py:243
  878.1 133.4 %copy-start.15 = (bf16[2,512,768]{2,1,0:T(8,128)(2,1)}, bf16[2,512,768]{2,1,0:T(8,128)(2,1)S(1)}, u32[]{:S(2)}) copy-start(bf16[2,512,768]{2,1,0:T(8,128)(2,1)S(1)} %convert.15) | copy-start | bytes 4718596
  1011.5 470.1 %all-reduce.14.cloned.1.call-start = ((), (), s32[]{:S(2)}) async-start(), calls=%async_computation.18 | async-start | bytes 28311552 | tf_op jit(solution)/shard_map/psum | solution.py:255
  1101.7 88.7 %copy-start.39 = (f32[1024]{0:T(1024)S(1)}, f32[1024]{0:T(1024)}, u32[]{:S(2)}) copy-start(f32[1024]{0:T(1024)} %copy-done.38) | copy-start | bytes 12292
  (57 other events, 347.4 us)
Sparse Core Ops, SparseCore 0:
  9.6 15.3 all-gather.15
  35.2 71.1 all-gather.19
  108.9 70.0 all-gather.17
  180.3 9.2 all-gather.21
  191.0 15.5 all-gather.23
  208.0 15.6 all-gather.25
  755.2 120.7 reduce-scatter.8
  879.2 120.7 reduce-scatter.6
  1002.8 9.8 reduce-scatter.12
  1014.9 18.9 reduce-scatter.14
  1036.3 19.0 reduce-scatter.16
  1057.7 16.8 reduce-scatter.10
  1081.0 400.6 all-reduce.13
where the time goes:
time: 1500 us
  waiting for transfers between devices  695 us (46%)
  matrix products  410 us (27%)
  other arithmetic  160 us (11%)
  local copies, waits for them, and re-layouts  111 us (7%)
  blocking collectives  103 us (7%)
  between operations  16.3 us (1%)
    psum x1, waiting for transfers between devices, body(): lax.psum((shards[0], shards[1], shards[2], shards[3], shards[4], shards[5...  287 us
    reduce_scatter x1, waiting for transfers between devices, body(): lax.psum_scatter(d_key_all, 'cp', scatter_dimension=1, tiled=True)  122 us
    reduce_scatter x1, waiting for transfers between devices, body(): lax.psum_scatter(d_value_all, 'cp', scatter_dimension=1, tiled=True)  88.8 us
    dot_general x4, matrix products, masked_scores(): jnp.einsum('qhd,khd->hqk', q_three, k_three, preferred_element_type=jnp.f...  86.3 us
    convert_element_type x2, other arithmetic, attend_back(): d_scores = (probs * (d_probs - delta)).astype(jnp.bfloat16)  82.8 us
    psum x1, blocking collectives, body(): lax.psum((shards[0], shards[1], shards[2], shards[3], shards[4], shards[5...  82.4 us
    dot_general x2, matrix products, attend_back(): jnp.einsum('qhd,khd->hqk', d_three, v_three, preferred_element_type=jnp.f...  75.1 us
    all_gather x1, waiting for transfers between devices, body(): lax.all_gather(value_loc, 'cp', axis=1, tiled=True)  72.5 us
  transfers between devices with their start and end apart: 13, of which 10 were waited for; matrix products, arithmetic and copies ran while one was open for 17% of the time, Pallas kernels for 0%

commit v1 on v0

--- a/solution.py
+++ b/solution.py
@@ -252,24 +252,23 @@
         lax.psum_scatter(dw_proj, "fsdp", scatter_dimension=0, tiled=True),
         lax.psum_scatter(db_proj, "fsdp", scatter_dimension=0, tiled=True),
     )
-    totals = lax.psum(
-        (
-            shards[0],
-            shards[1],
-            shards[2],
-            shards[3],
-            shards[4],
-            shards[5],
-            shards[6],
-            shards[7],
-            shards[8],
-            shards[9],
-            shards[10],
-            shards[11],
-            shards[12],
-        ),
-        ("cp", "rep"),
-    )
+    totals = (
+        shards[0],
+        shards[1],
+        shards[2],
+        shards[3],
+        shards[4],
+        shards[5],
+        shards[6],
+        shards[7],
+        shards[8],
+        shards[9],
+        shards[10],
+        shards[11],
+        shards[12],
+    )
+    for src_i in ("rep", "cp"):
+        totals = lax.psum(totals, src_i)
     return (
         layer_out,
         tokens_grad,

time: 1500 us -> 1850 us (1.23)
  waiting for transfers between devices: 695 us -> 1090 us
  blocking collectives: 103 us -> 53.8 us
    psum x1 -> x2, waiting for transfers between devices: 287 us -> 680 us  [body(): totals = lax.psum(totals, src_i)]
    psum x1 -> x2, blocking collectives: 82.4 us -> 33.7 us  [body(): totals = lax.psum(totals, src_i)]
  transfers between devices with their start and end apart: 13 -> 14, of which waited for: 10 -> 11; matrix products, arithmetic and copies ran while one was open for 17% -> 14% of each run, Pallas kernels for 0% -> 0%
where the time goes in v1:
time: 1850 us
  waiting for transfers between devices  1090 us (59%)
  matrix products  411 us (22%)
  other arithmetic  160 us (9%)
  local copies, waits for them, and re-layouts  111 us (6%)
  blocking collectives  53.8 us (3%)
    psum x2, waiting for transfers between devices, body(): totals = lax.psum(totals, src_i)  680 us
    reduce_scatter x1, waiting for transfers between devices, body(): lax.psum_scatter(d_key_all, 'cp', scatter_dimension=1, tiled=True)  122 us
    reduce_scatter x1, waiting for transfers between devices, body(): lax.psum_scatter(d_value_all, 'cp', scatter_dimension=1, tiled=True)  89 us
    dot_general x4, matrix products, masked_scores(): jnp.einsum('qhd,khd->hqk', q_three, k_three, preferred_element_type=jnp.f...  86.3 us
    convert_element_type x2, other arithmetic, attend_back(): d_scores = (probs * (d_probs - delta)).astype(jnp.bfloat16)  82.8 us
    dot_general x2, matrix products, attend_back(): jnp.einsum('qhd,khd->hqk', d_three, v_three, preferred_element_type=jnp.f...  75.1 us
    all_gather x1, waiting for transfers between devices, body(): lax.all_gather(value_loc, 'cp', axis=1, tiled=True)  72.5 us
    all_gather x1, waiting for transfers between devices, body(): lax.all_gather(key_loc, 'cp', axis=1, tiled=True)  56.3 us
  transfers between devices with their start and end apart: 14, of which 11 were waited for; matrix products, arithmetic and copies ran while one was open for 14% of the time, Pallas kernels for 0%

profile of v1, /device:TPU:0, one launch (start us, length us, event | category | flops | bytes accessed | tf_op | source)
XLA Modules:
  0.0 1845.9 jit_solution(9593175190271098832)
XLA Ops:
  50.2 56.3 %all-gather.20.cloned.1.call-done = bf16[2,2048,768]{1,2,0:T(8,128)(2,1)} async-done(((bf16[2,512,768]{1,2,0:T(8,128)(2,1)}), bf16[2,2048,768]{1,2,0:T(8,128)(2,1)}) %all-gather.20.cloned.1.call-update) | async-done | bytes 6291472 | tf_op jit(solution)/shard_map/all_gather | solution.py:89
  106.5 72.5 %all-gather.18.cloned.1.call-done = bf16[2,2048,768]{1,2,0:T(8,128)(2,1)} async-done(((bf16[2,512,768]{1,2,0:T(8,128)(2,1)}), bf16[2,2048,768]{1,2,0:T(8,128)(2,1)}) %all-gather.18.cloned.1.call-update) | async-done | bytes 6291472 | tf_op jit(solution)/shard_map/all_gather | solution.py:90
  178.9 155.5 %while.34 = (s32[]{:T(128)}, bf16[2,512,768]{2,1,0:T(8,128)(2,1)}, f32[2,12,512]{2,1,0:T(8,128)S(1)}, bf16[2,2048,768]{1,2,0:T(8,128)(2,1)}, s32[2,2048]{1,0:T(2...) while((s32[]{:T(128)}, bf16[2,512,768]{2,1,0:T(8,128)(2,1)}, ...), condition=%wide.region_5.6_spmd.clone, body=%wide.region_2.5_spmd.clone.sunk | while | flops 3375753728 | bytes 197388496 | solution.py:127
  188.6 23.9 %fusion.106 = (f32[12,512]{1,0:T(8,128)S(1)}, f32[12,512,2048]{2,1,0:T(8,128)}) fusion(pred[512,2048]{1,0:T(8,128)(4,1)} %fusion.105, bf16[512,12,64]{0,2,1:T(8,128)(2,1)} %bitcast.170, bf16[2048,12,64]{0,2,1:T(8,128)(2,1)S(1)} %bitcast.165), kind=kOutput, calls=%fused_computation.5.clone.1 | convolution fusion | flops 1648355328 | bytes 55336960 | tf_op jit(solution)/shard_map/while/body/eval_jaxpr/qhd,khd->hqk/dot_general | solution.py:99
  212.5 24.5 %fusion.107 = f32[12,512]{1,0:T(8,128)S(1)} fusion(f32[12,512,2048]{2,1,0:T(8,128)} %get-tuple-element.696, f32[12,512]{1,0:T(8,128)S(1)} %get-tuple-element.697, pred[512,2048]{1,0:T(8,128)(4,1)} %fusion.105), kind=kLoop, calls=%fused_computation.6.clone.1 | loop fusion | flops 50325504 | bytes 51429376 | tf_op jit(solution)/shard_map/while/body/eval_jaxpr/reduce_sum | solution.py:114
  237.1 20.2 %fusion.108 = bf16[12,64,512]{2,1,0:T(8,128)(2,1)S(1)} fusion(bf16[2048,12,64]{0,2,1:T(8,128)(2,1)S(1)} %bitcast.174, f32[12,512,2048]{2,1,0:T(8,128)} %get-tuple-element.696, f32[12,512]{1,0:T(8,128)S(1)} %fusion.107, f32[12,512]{1,0:T(8,128)S(1)} %get-tuple-element.697, pred[512,2048]{1,0:T(8,128)(4,1)S(1)} %copy-done), kind=kOutput, calls=%fused_computation.10.clone.1 | convolution fusion | flops 1673920512 | bytes 55361536 | tf_op jit(solution)/shard_map/while/body/eval_jaxpr/hqk,khd->qhd/dot_general | solution.py:116
  268.2 21.5 %fusion.106 = (f32[12,512]{1,0:T(8,128)S(1)}, f32[12,512,2048]{2,1,0:T(8,128)}) fusion(pred[512,2048]{1,0:T(8,128)(4,1)} %fusion.105, bf16[512,12,64]{0,2,1:T(8,128)(2,1)} %bitcast.170, bf16[2048,12,64]{0,2,1:T(8,128)(2,1)S(1)} %bitcast.165), kind=kOutput, calls=%fused_computation.5.clone.1 | convolution fusion | flops 1648355328 | bytes 55336960 | tf_op jit(solution)/shard_map/while/body/eval_jaxpr/qhd,khd->hqk/dot_general | solution.py:99
  289.7 22.9 %fusion.107 = f32[12,512]{1,0:T(8,128)S(1)} fusion(f32[12,512,2048]{2,1,0:T(8,128)} %get-tuple-element.696, f32[12,512]{1,0:T(8,128)S(1)} %get-tuple-element.697, pred[512,2048]{1,0:T(8,128)(4,1)} %fusion.105), kind=kLoop, calls=%fused_computation.6.clone.1 | loop fusion | flops 50325504 | bytes 51429376 | tf_op jit(solution)/shard_map/while/body/eval_jaxpr/reduce_sum | solution.py:114
  312.5 20.2 %fusion.108 = bf16[12,64,512]{2,1,0:T(8,128)(2,1)S(1)} fusion(bf16[2048,12,64]{0,2,1:T(8,128)(2,1)S(1)} %bitcast.174, f32[12,512,2048]{2,1,0:T(8,128)} %get-tuple-element.696, f32[12,512]{1,0:T(8,128)S(1)} %fusion.107, f32[12,512]{1,0:T(8,128)S(1)} %get-tuple-element.697, pred[512,2048]{1,0:T(8,128)(4,1)S(1)} %copy-done), kind=kOutput, calls=%fused_computation.10.clone.1 | convolution fusion | flops 1673920512 | bytes 55361536 | tf_op jit(solution)/shard_map/while/body/eval_jaxpr/hqk,khd->qhd/dot_general | solution.py:116
  379.8 375.4 %while.35 = (s32[]{:T(128)}, bf16[2,512,768]{2,1,0:T(8,128)(2,1)}, f32[2,2048,768]{2,1,0:T(8,128)}, f32[2,2048,768]{2,1,0:T(8,128)}, bf16[2,2048,768]{1,2,0:T(8,...) while((s32[]{:T(128)}, bf16[2,512,768]{2,1,0:T(8,128)(2,1)}, ...), condition=%wide.region_12.13_spmd.clone, body=%wide.region_10.12_spmd.clone.sunk | while | flops 8247306752 | bytes 519514368 | solution.py:218
  392.8 20.5 %fusion.119 = f32[12,512,2048]{2,1,0:T(8,128)} fusion(bf16[512,12,64]{0,2,1:T(8,128)(2,1)} %bitcast.167, bf16[2048,12,64]{0,2,1:T(8,128)(2,1)S(1)} %bitcast.162), kind=kOutput, calls=%fused_computation.114.clone.1 | convolution fusion | flops 1610612736 | bytes 54263808 | tf_op jit(solution)/shard_map/while/body/eval_jaxpr/qhd,khd->hqk/dot_general | solution.py:99
  413.3 23.1 %fusion.121 = f32[12,64,2048]{2,1,0:T(8,128)} fusion(bf16[512,12,64]{0,2,1:T(8,128)(2,1)} %bitcast.172, f32[12,512,2048]{2,1,0:T(8,128)} %fusion.119, f32[12,512]{1,0:T(8,128)S(1)} %dynamic-slice_bitcast_fusion.2, pred[512,2048]{1,0:T(8,128)(4,1)} %fusion.120), kind=kOutput, calls=%fused_computation.24.clone.1 | convolution fusion | flops 1660944384 | bytes 58482688 | tf_op jit(solution)/shard_map/while/body/eval_jaxpr/hqk,qhd->khd/dot_general | solution.py:209
  443.1 37.6 %multiply_reduce_fusion.5 = (f32[12,512]{1,0:T(8,128)S(1)}, f32[12,512,2048]{2,1,0:T(8,128)}) fusion(f32[12,512,2048]{2,1,0:T(8,128)} %fusion.119, f32[12,512]{1,0:T(8,128)S(1)} %dynamic-slice_bitcast_fusion.2, pred[512,2048]{1,0:T(8,128)(4,1)} %fusion.120, bf16[512,12,64]{0,2,1:T(8,128)(2,1)} %bitcast.173, bf16[2048,12,64]{0,2,1:T(8,128)(2,1)} %bitcast.166), kind=kOutput, calls=%fused_computation.21.clone.1 | convolution fusion | flops 1673521152 | bytes 105693184 | tf_op jit(solution)/shard_map/while/body/eval_jaxpr/qhd,khd->hqk/dot_general | solution.py:188
  480.6 41.4 %multiply_convert_fusion.5 = bf16[12,512,2048]{2,1,0:T(8,128)(2,1)} fusion(f32[12,512,2048]{2,1,0:T(8,128)} %get-tuple-element.710, f32[12,512,2048]{2,1,0:T(8,128)} %fusion.119, f32[12,512]{1,0:T(8,128)S(1)} %get-tuple-element.711, f32[12,512]{1,0:T(8,128)S(1)} %dynamic-slice_bitcast_fusion.2, pred[512,2048]{1,0:T(8,128)(4,1)} %fusion.120), kind=kLoop, calls=%fused_computation.20.clone.1 | loop fusion | flops 75497472 | bytes 126926848 | tf_op jit(solution)/shard_map/while/body/eval_jaxpr/convert_element_type | solution.py:190
  578.9 20.5 %fusion.119 = f32[12,512,2048]{2,1,0:T(8,128)} fusion(bf16[512,12,64]{0,2,1:T(8,128)(2,1)} %bitcast.167, bf16[2048,12,64]{0,2,1:T(8,128)(2,1)S(1)} %bitcast.162), kind=kOutput, calls=%fused_computation.114.clone.1 | convolution fusion | flops 1610612736 | bytes 54263808 | tf_op jit(solution)/shard_map/while/body/eval_jaxpr/qhd,khd->hqk/dot_general | solution.py:99
  599.4 23.1 %fusion.121 = f32[12,64,2048]{2,1,0:T(8,128)} fusion(bf16[512,12,64]{0,2,1:T(8,128)(2,1)} %bitcast.172, f32[12,512,2048]{2,1,0:T(8,128)} %fusion.119, f32[12,512]{1,0:T(8,128)S(1)} %dynamic-slice_bitcast_fusion.2, pred[512,2048]{1,0:T(8,128)(4,1)} %fusion.120), kind=kOutput, calls=%fused_computation.24.clone.1 | convolution fusion | flops 1660944384 | bytes 58482688 | tf_op jit(solution)/shard_map/while/body/eval_jaxpr/hqk,qhd->khd/dot_general | solution.py:209
  629.2 37.6 %multiply_reduce_fusion.5 = (f32[12,512]{1,0:T(8,128)S(1)}, f32[12,512,2048]{2,1,0:T(8,128)}) fusion(f32[12,512,2048]{2,1,0:T(8,128)} %fusion.119, f32[12,512]{1,0:T(8,128)S(1)} %dynamic-slice_bitcast_fusion.2, pred[512,2048]{1,0:T(8,128)(4,1)} %fusion.120, bf16[512,12,64]{0,2,1:T(8,128)(2,1)} %bitcast.173, bf16[2048,12,64]{0,2,1:T(8,128)(2,1)} %bitcast.166), kind=kOutput, calls=%fused_computation.21.clone.1 | convolution fusion | flops 1673521152 | bytes 105693184 | tf_op jit(solution)/shard_map/while/body/eval_jaxpr/qhd,khd->hqk/dot_general | solution.py:188
  666.8 41.4 %multiply_convert_fusion.5 = bf16[12,512,2048]{2,1,0:T(8,128)(2,1)} fusion(f32[12,512,2048]{2,1,0:T(8,128)} %get-tuple-element.710, f32[12,512,2048]{2,1,0:T(8,128)} %fusion.119, f32[12,512]{1,0:T(8,128)S(1)} %get-tuple-element.711, f32[12,512]{1,0:T(8,128)S(1)} %dynamic-slice_bitcast_fusion.2, pred[512,2048]{1,0:T(8,128)(4,1)} %fusion.120), kind=kLoop, calls=%fused_computation.20.clone.1 | loop fusion | flops 75497472 | bytes 126926848 | tf_op jit(solution)/shard_map/while/body/eval_jaxpr/convert_element_type | solution.py:190
  787.2 89.0 %reduce-scatter.9.cloned.1.call-done = f32[2,512,768]{2,1,0:T(8,128)} async-done(((f32[2,2048,768]{2,1,0:T(8,128)}), f32[2,512,768]{2,1,0:T(8,128)}) %reduce-scatter.9.cloned.1.call-update) | async-done | bytes 3145744 | tf_op jit(solution)/shard_map/reduce_scatter | solution.py:223
  878.2 121.8 %reduce-scatter.7.cloned.1.call-done = f32[2,512,768]{2,1,0:T(8,128)} async-done(((f32[2,2048,768]{2,1,0:T(8,128)}), f32[2,512,768]{2,1,0:T(8,128)}) %reduce-scatter.7.cloned.1.call-update) | async-done | bytes 3145744 | tf_op jit(solution)/shard_map/reduce_scatter | solution.py:222
  1012.8 21.2 %reduce-scatter.15.cloned.1.call-done = f32[384,3072]{1,0:T(8,128)} async-done(((f32[768,3072]{1,0:T(8,128)}), f32[384,3072]{1,0:T(8,128)}) %reduce-scatter.15.cloned.1.call-update) | async-done | bytes 4718608 | tf_op jit(solution)/shard_map/reduce_scatter | solution.py:250
  1034.0 21.5 %reduce-scatter.17.cloned.1.call-done = f32[1536,768]{1,0:T(8,128)} async-done(((f32[3072,768]{1,0:T(8,128)}), f32[1536,768]{1,0:T(8,128)}) %reduce-scatter.17.cloned.1.call-update) | async-done | bytes 4718608 | tf_op jit(solution)/shard_map/reduce_scatter | solution.py:252
  1074.7 482.9 %all-reduce.17.cloned.1.call-done = (f32[384,2304]{1,0:T(8,128)}, f32[384,768]{1,0:T(8,128)}, f32[384,3072]{1,0:T(8,128)}, f32[1536,768]{1,0:T(8,128)}) async-done(((f32[384,2304]{1,0:T(8,128)}, f32[384,768]{1,0:T(8,128)}, f32[384,3072]{1,0:T(8,128)}, f32[1536,768]{1,0:T(8,128)}), (f32[384,2304]{1,0:T(8,128)}, f32[384,768]{1,0:T(8,128)}, f32[384,3072]{1,0:T(8,128)}, ...) | async-done | bytes 14155792 | tf_op jit(solution)/shard_map/psum | solution.py:271
  1631.1 197.3 %all-reduce.19.cloned.1.call-done = (f32[384,2304]{1,0:T(8,128)}, f32[384,768]{1,0:T(8,128)}, f32[384,3072]{1,0:T(8,128)}, f32[1536,768]{1,0:T(8,128)}) async-done(((f32[384,2304]{1,0:T(8,128)}, f32[384,768]{1,0:T(8,128)}, f32[384,3072]{1,0:T(8,128)}, f32[1536,768]{1,0:T(8,128)}), (f32[384,2304]{1,0:T(8,128)}, f32[384,768]{1,0:T(8,128)}, f32[384,3072]{1,0:T(8,128)}, ...) | async-done | bytes 14155792 | tf_op jit(solution)/shard_map/psum | solution.py:271
  (323 shorter events, 385.0 us)
Async XLA Ops:
  7.2 17.8 all-gather.16.cloned.1.call-start
  7.9 98.5 %all-gather.20.cloned.1.call-start = ((), (), s32[]{:S(2)}) async-start(), calls=%async_computation.8 | async-start | bytes 7864320 | tf_op jit(solution)/shard_map/all_gather | solution.py:89
  35.1 143.8 %all-gather.18.cloned.1.call-start = ((), (), s32[]{:S(2)}) async-start(), calls=%async_computation.7 | async-start | bytes 7864320 | tf_op jit(solution)/shard_map/all_gather | solution.py:90
  36.8 297.7 %all-gather.22.cloned.1.call-start = ((), (), s32[]{:S(2)}) async-start(), calls=%async_computation.9 | async-start | bytes 1769472 | tf_op jit(solution)/shard_map/all_gather | solution.py:65
  37.4 141.6 %copy-start.23 = (s32[2,2048]{1,0:T(2,128)S(1)}, s32[2,2048]{1,0:T(2,128)}, u32[]{:S(2)}) copy-start(s32[2,2048]{1,0:T(2,128)} %param.21) | copy-start | bytes 49156
  37.4 301.5 %all-gather.24.cloned.1.call-start = ((), (), s32[]{:S(2)}) async-start(), calls=%async_computation.10 | async-start | bytes 7077888 | tf_op jit(solution)/shard_map/all_gather | solution.py:69
  38.0 311.9 %all-gather.26.cloned.1.call-start = ((), (), s32[]{:S(2)}) async-start(), calls=%async_computation.11 | async-start | bytes 7077888 | tf_op jit(solution)/shard_map/all_gather | solution.py:71
  38.5 837.6 %reduce-scatter.9.cloned.1.call-start = ((), (), s32[]{:S(2)}) async-start(), calls=%async_computation.13 | async-start | bytes 15728640 | tf_op jit(solution)/shard_map/reduce_scatter | solution.py:223
  178.9 155.5 %copy-start.46 = (f32[768]{0:T(1024)S(1)}, f32[768]{0:T(1024)}, u32[]{:S(2)}) copy-start(f32[768]{0:T(1024)} %reshape.447) | copy-start | bytes 9220
  212.5 24.5 %copy-start = (pred[512,2048]{1,0:T(8,128)(4,1)S(1)}, pred[512,2048]{1,0:T(8,128)(4,1)}, u32[]{:S(2)}) copy-start(pred[512,2048]{1,0:T(8,128)(4,1)} %fusion.105) | copy-start | bytes 3145732 | tf_op jit(solution)/shard_map/while
  212.5 24.5 %copy-start.3 = (bf16[1,2048,768]{1,2,0:T(8,128)(2,1)S(1)}, bf16[1,2048,768]{1,2,0:T(8,128)(2,1)}, u32[]{:S(2)}) copy-start(bf16[1,2048,768]{1,2,0:T(8,128)(2,1)} %get-tuple-element.694) | copy-start | bytes 9437188 | tf_op jit(solution)/shard_map/while
  289.6 22.9 %copy-start.3 = (bf16[1,2048,768]{1,2,0:T(8,128)(2,1)S(1)}, bf16[1,2048,768]{1,2,0:T(8,128)(2,1)}, u32[]{:S(2)}) copy-start(bf16[1,2048,768]{1,2,0:T(8,128)(2,1)} %get-tuple-element.694) | copy-start | bytes 9437188 | tf_op jit(solution)/shard_map/while
  338.3 36.4 %copy-start.6 = (f32[1024,768]{1,0:T(8,128)}, f32[1024,768]{1,0:T(8,128)S(1)}, u32[]{:S(2)}) copy-start(f32[1024,768]{1,0:T(8,128)S(1)} %get-tuple-element.565) | copy-start | bytes 9437188
  338.3 36.4 %copy-start.24 = (f32[1024]{0:T(1024)}, f32[1024]{0:T(1024)S(1)}, u32[]{:S(2)}) copy-start(f32[1024]{0:T(1024)S(1)} %broadcast_multiply_fusion) | copy-start | bytes 12292
  338.8 35.9 %copy-start.26 = (f32[1024]{0:T(1024)}, f32[1024]{0:T(1024)S(1)}, u32[]{:S(2)}) copy-start(f32[1024]{0:T(1024)S(1)} %fusion.36) | copy-start | bytes 12292
  755.2 244.8 %reduce-scatter.7.cloned.1.call-start = ((), (), s32[]{:S(2)}) async-start(), calls=%async_computation.12 | async-start | bytes 15728640 | tf_op jit(solution)/shard_map/reduce_scatter | solution.py:222
  756.0 256.8 %reduce-scatter.13.cloned.1.call-start = ((), (), s32[]{:S(2)}) async-start(), calls=%async_computation.15 | async-start | bytes 3538944 | tf_op jit(solution)/shard_map/reduce_scatter | solution.py:246
  761.0 273.0 %reduce-scatter.15.cloned.1.call-start = ((), (), s32[]{:S(2)}) async-start(), calls=%async_computation.16 | async-start | bytes 14155776 | tf_op jit(solution)/shard_map/reduce_scatter | solution.py:250
  772.7 282.7 %reduce-scatter.17.cloned.1.call-start = ((), (), s32[]{:S(2)}) async-start(), calls=%async_computation.17 | async-start | bytes 14155776 | tf_op jit(solution)/shard_map/reduce_scatter | solution.py:252
  787.1 287.5 %reduce-scatter.11.cloned.1.call-start = ((), (), s32[]{:S(2)}) async-start(), calls=%async_computation.14 | async-start | bytes 10616832 | tf_op jit(solution)/shard_map/reduce_scatter | solution.py:243
  878.2 133.5 %copy-start.15 = (bf16[2,512,768]{2,1,0:T(8,128)(2,1)}, bf16[2,512,768]{2,1,0:T(8,128)(2,1)S(1)}, u32[]{:S(2)}) copy-start(bf16[2,512,768]{2,1,0:T(8,128)(2,1)S(1)} %convert.15) | copy-start | bytes 4718596
  1011.7 545.8 %all-reduce.17.cloned.1.call-start = ((), (), s32[]{:S(2)}) async-start(), calls=%async_computation.18 | async-start | bytes 28311552 | tf_op jit(solution)/shard_map/psum | solution.py:271
  1074.6 753.7 %all-reduce.19.cloned.1.call-start = ((), (), s32[]{:S(2)}) async-start(), calls=%async_computation.19 | async-start | bytes 28311552 | tf_op jit(solution)/shard_map/psum | solution.py:271
  1586.2 40.0 %copy-start.39 = (f32[1024]{0:T(1024)S(1)}, f32[1024]{0:T(1024)}, u32[]{:S(2)}) copy-start(f32[1024]{0:T(1024)} %copy-done.38) | copy-start | bytes 12292
  (58 other events, 377.2 us)
Sparse Core Ops, SparseCore 0:
  9.6 15.3 all-gather.15
  35.2 71.1 all-gather.19
  108.9 70.0 all-gather.17
  180.3 9.2 all-gather.21
  191.0 15.5 all-gather.23
  208.0 15.6 all-gather.25
  755.3 120.7 reduce-scatter.8
  879.3 120.7 reduce-scatter.6
  1002.9 9.8 reduce-scatter.12
  1015.0 18.9 reduce-scatter.14
  1036.4 19.0 reduce-scatter.16
  1057.7 16.8 reduce-scatter.10
  1077.5 479.9 all-reduce.16
  1561.3 266.9 all-reduce.18
